TPU v7x, 32 devices: a whole 2x2x4 slice. The times are simulated.
32 devices in a mesh: shard: 2 (over y), ctx: 4 (over z), tp: 4 (over x, core).
Axes of the slice: x: 2, y: 2, z: 4, core: 2. Of those that a mesh axis runs over, the one named last changes fastest.
Arguments:
- inputs: bfloat16 [2, 4096, 768], P('shard', 'ctx'), may hold values from -6 to 6
- lengths: int32 [2], P('shard'), may hold values from 1024 to 4096, as said below
- global_blocks: int32 [2, 2], P('shard'), may hold values from 0 to 15, as said below
- random_blocks: int32 [2, 64, 3], P('shard', 'ctx'), may hold values from 0 to 63
- master_blocks: float32 [768, 96, 96], P(('shard', 'ctx', 'tp'))
- outer_vectors: float32 [6, 768], replicated
- inner_biases: float32 [4, 1152], P('tp'), may hold values from -4 to 4
- left_stats: float32 [768, 96, 96], P(('shard', 'ctx', 'tp')), as said below
- right_stats: float32 [768, 96, 96], P(('shard', 'ctx', 'tp')), as said below
- left_roots: float32 [768, 96, 96], P(('shard', 'ctx', 'tp')), as said below
- right_roots: float32 [768, 96, 96], P(('shard', 'ctx', 'tp')), as said below
- cotangent: bfloat16 [2, 4096, 768], P('shard', 'ctx'), may hold values from -6 to 6
Outputs:
- output: bfloat16 [2, 4096, 768], P('shard', 'ctx')
- input_grad: bfloat16 [2, 4096, 768], P('shard', 'ctx')
- block_grads: float32 [768, 96, 96], P(('shard', 'ctx', 'tp'))
- outer_grads: float32 [6, 768], P(None, ('shard', 'ctx'))
- inner_grads: float32 [4, 1152], P('tp', ('shard', 'ctx'))
- maxima: float32 [12], P('tp')
- left_new: float32 [768, 96, 96], P(('shard', 'ctx', 'tp'))
- right_new: float32 [768, 96, 96], P(('shard', 'ctx', 'tp'))
- new_blocks: float32 [768, 96, 96], P(('shard', 'ctx', 'tp'))
- new_outer: float32 [6, 768], P(None, ('shard', 'ctx'))
- new_inner: float32 [4, 1152], P('tp', ('shard', 'ctx'))
Inputs may be any that keep to these rules, and one draw needn't show every extreme that they name: `lengths`: sequence 0 holds 4096 valid tokens. `global_blocks`: the two ids of a sequence differ. `left_stats`: each block is symmetric. `right_stats`: each block is symmetric. `left_roots`: each block is symmetric. `right_roots`: each block is symmetric.
All inputs are finite; a program needn't handle non-finite values.
Results may differ from a plain program's by a relative error of at most 0.018.
Values may be sent and summed in bfloat16 or wider, within the bound.
No kernel may reach another device: no remote copies, remote signals or barrier semaphores. Data moves between devices by JAX's collectives and lax.ppermute only.
A program may use at most 192 MiB of HBM per device.

v0:
```python
import jax
import jax.numpy as jnp
from jax import lax
from jax.sharding import PartitionSpec as P

D = 768
HEADS = 12
HEAD = 64
FF = 3072
BLOCK = 64
SEQ = 4096
PB = 96
eps_norm = 1e-06
tau_clip = 9.0
rate_matrix = 0.3
rate_vector = 0.001
neg_large = -1e30
high = lax.Precision.HIGHEST


def layer_norm(values, gain, shift):
    mean_val = jnp.mean(values, axis=-1, keepdims=True)
    centred = values - mean_val
    var_val = jnp.mean(centred * centred, axis=-1, keepdims=True)
    return centred * lax.rsqrt(var_val + eps_norm) * gain + shift


def gelu_tanh(values):
    return jax.nn.gelu(values, approximate=True)


def to_grid(blocks, row_count, col_count):
    shaped = blocks.reshape(row_count // PB, col_count // PB, PB, PB)
    return shaped.transpose(0, 2, 1, 3).reshape(row_count, col_count)


def from_grid(matrix):
    row_count, col_count = matrix.shape
    shaped = matrix.reshape(row_count // PB, PB, col_count // PB, PB)
    return shaped.transpose(0, 2, 1, 3).reshape(-1, PB, PB)


def unpack_weights(whole, head_cols, unit_count):
    first_end = D // PB * (3 * head_cols // PB)
    second_end = first_end + head_cols // PB * (D // PB)
    third_end = second_end + D // PB * (unit_count // PB)
    return (
        to_grid(whole[:first_end], D, 3 * head_cols),
        to_grid(whole[first_end:second_end], head_cols, D),
        to_grid(whole[second_end:third_end], D, unit_count),
        to_grid(whole[third_end:], unit_count, D),
    )


def block_layout(slot_length, global_ids, random_ids, first_block, rows_blocks, block_count):
    rows = first_block + jnp.arange(rows_blocks, dtype=jnp.int32)
    window = jnp.stack([rows - 1, rows, rows + 1], axis=1)
    globals_row = jnp.broadcast_to(global_ids[None, :], (rows_blocks, 2))
    listed = jnp.concatenate([window, globals_row, random_ids], axis=1)
    inside = (listed >= 0) & (listed < block_count)
    clipped = jnp.clip(listed, 0, block_count - 1)
    key_pos = listed[:, :, None] * BLOCK + jnp.arange(BLOCK, dtype=jnp.int32)[None, None, :]
    key_mask = (inside[:, :, None] & (key_pos < slot_length)).reshape(rows_blocks, -1)
    query_pos = (first_block * BLOCK + jnp.arange(rows_blocks * BLOCK, dtype=jnp.int32)).reshape(
        rows_blocks, BLOCK
    )
    return (clipped, key_mask, query_pos < slot_length)


def pick_blocks(full_rows, clipped, head_count):
    block_count = full_rows.shape[0] // BLOCK
    picked = full_rows.reshape(block_count, BLOCK, -1)[clipped]
    return picked.reshape(clipped.shape[0], clipped.shape[1] * BLOCK, head_count, HEAD)


def attend_scores(query_blocks, key_blocks):
    return jnp.einsum(
        "lqhd,lkhd->lhqk", query_blocks, key_blocks, preferred_element_type=jnp.float32
    ) * HEAD ** (-0.5)


def probs_again(query_blocks, d_out_blocks, key_blocks, value_blocks, key_mask, lse_blk):
    raw_scores = attend_scores(query_blocks, key_blocks)
    probs = jnp.exp(jnp.where(key_mask[:, None, None, :], raw_scores, neg_large) - lse_blk)
    d_probs = jnp.einsum(
        "lqhd,lkhd->lhqk", d_out_blocks, value_blocks, preferred_element_type=jnp.float32
    )
    return (probs, d_probs)


def group_back(
    query_blocks,
    d_out_blocks,
    key_src,
    value_src,
    clipped,
    key_mask,
    lse_blk,
    delta_blk,
    block_count,
):
    rows_blocks, _, heads_here, _ = query_blocks.shape
    head_cols = heads_here * HEAD
    key_blocks = pick_blocks(key_src, clipped, heads_here)
    value_blocks = pick_blocks(value_src, clipped, heads_here)
    probs, d_probs = probs_again(
        query_blocks, d_out_blocks, key_blocks, value_blocks, key_mask, lse_blk
    )
    delta_blk = jnp.sum(probs * d_probs, axis=-1, keepdims=True)
    d_scores = (probs * (d_probs - delta_blk)).astype(jnp.bfloat16)
    d_query = jnp.einsum(
        "lhqk,lkhd->lqhd", d_scores, key_blocks, preferred_element_type=jnp.float32
    ) * HEAD ** (-0.5)
    d_key_blocks = jnp.einsum(
        "lhqk,lqhd->lkhd", d_scores, query_blocks, preferred_element_type=jnp.float32
    ) * HEAD ** (-0.5)
    d_value_blocks = jnp.einsum(
        "lhqk,lqhd->lkhd",
        probs.astype(jnp.bfloat16),
        d_out_blocks,
        preferred_element_type=jnp.float32,
    )
    listed_count = clipped.shape[1]
    d_key_full = (
        jnp.zeros((block_count, BLOCK, head_cols), jnp.float32)
        .at[clipped]
        .add(d_key_blocks.reshape(rows_blocks, listed_count, BLOCK, head_cols))
    )
    d_value_full = (
        jnp.zeros((block_count, BLOCK, head_cols), jnp.float32)
        .at[clipped]
        .add(d_value_blocks.reshape(rows_blocks, listed_count, BLOCK, head_cols))
    )
    return (
        d_query.reshape(-1, head_cols),
        d_key_full.reshape(-1, head_cols),
        d_value_full.reshape(-1, head_cols),
    )


def per_device(
    inputs,
    lengths,
    global_blocks,
    random_blocks,
    master_blocks,
    outer_vectors,
    inner_biases,
    left_stats,
    right_stats,
    left_roots,
    right_roots,
    cotangent,
):
    tensor_count = lax.axis_size("tp")
    owner_count = lax.axis_size(("shard", "ctx"))
    heads_here = HEADS // tensor_count
    head_cols = heads_here * HEAD
    unit_count = FF // tensor_count
    slot_count, ctx_tokens, _ = inputs.shape
    rows_blocks = ctx_tokens // BLOCK
    block_count = SEQ // BLOCK
    ctx_index = lax.axis_index("ctx")
    owner_index = lax.axis_index(("shard", "ctx"))
    gathered = lax.all_gather(
        master_blocks.astype(jnp.bfloat16), ("shard", "ctx"), axis=0, tiled=True
    )
    w_qkv, w_out, w_up, w_down = unpack_weights(gathered, head_cols, unit_count)
    flat_in = inputs.reshape(-1, D)
    inner_row = inner_biases[0]
    q_bias = inner_row[:head_cols]
    v_bias = inner_row[head_cols : 2 * head_cols]
    up_bias = inner_row[2 * head_cols :]
    projected = jnp.dot(flat_in, w_qkv, preferred_element_type=jnp.float32)
    queries = (projected[:, :head_cols] + q_bias).astype(jnp.bfloat16)
    key_rows = (
        projected[:, head_cols : 2 * head_cols]
        .astype(jnp.bfloat16)
        .reshape(slot_count, ctx_tokens, head_cols)
    )
    value_rows = (
        (projected[:, 2 * head_cols :] + v_bias)
        .astype(jnp.bfloat16)
        .reshape(slot_count, ctx_tokens, head_cols)
    )
    keys_all, values_all = (
        lax.all_gather(key_rows, "ctx", axis=1, tiled=True),
        lax.all_gather(value_rows, "ctx", axis=1, tiled=True),
    )
    query_slots = queries.reshape(slot_count, ctx_tokens, head_cols)
    peak_logit = jnp.full((heads_here,), neg_large, jnp.float32)
    slot_index = 0
    clipped, key_mask, query_mask = block_layout(
        lengths[slot_index],
        global_blocks[slot_index],
        random_blocks[slot_index],
        ctx_index * rows_blocks,
        rows_blocks,
        block_count,
    )
    layouts = [(clipped, key_mask)]
    query_blocks = query_slots[slot_index].reshape(rows_blocks, BLOCK, heads_here, HEAD)
    key_blocks = pick_blocks(keys_all[slot_index], clipped, heads_here)
    value_blocks = pick_blocks(values_all[slot_index], clipped, heads_here)
    raw_scores = attend_scores(query_blocks, key_blocks)
    both_mask = key_mask[:, None, None, :] & query_mask[:, None, :, None]
    peak_logit = jnp.maximum(
        peak_logit, jnp.max(jnp.where(both_mask, raw_scores, neg_large), axis=(0, 2, 3))
    )
    masked = jnp.where(key_mask[:, None, None, :], raw_scores, neg_large)
    row_top = jnp.max(masked, axis=-1, keepdims=True)
    shifted = jnp.exp(masked - row_top)
    row_total = jnp.sum(shifted, axis=-1, keepdims=True)
    probs = shifted / row_total
    lse_list = [row_top + jnp.log(row_total)]
    attended = jnp.einsum(
        "lhqk,lkhd->lqhd",
        probs.astype(jnp.bfloat16),
        value_blocks,
        preferred_element_type=jnp.float32,
    )
    attended_list = attended.reshape(ctx_tokens, head_cols)
    attended_low = attended_list.astype(jnp.bfloat16)
    branch = (
        lax.psum(jnp.dot(attended_low, w_out, preferred_element_type=jnp.float32), "tp")
        + outer_vectors[0]
    )
    hidden_in = flat_in.astype(jnp.float32) + branch
    x_first = layer_norm(hidden_in, outer_vectors[2], outer_vectors[3])
    x_first_low = x_first.astype(jnp.bfloat16)
    gate_pre = jnp.dot(x_first_low, w_up, preferred_element_type=jnp.float32) + up_bias
    act_low = gelu_tanh(gate_pre).astype(jnp.bfloat16)
    ff_out = (
        lax.psum(jnp.dot(act_low, w_down, preferred_element_type=jnp.float32), "tp")
        + outer_vectors[1]
    )
    mixed_sum = x_first + ff_out
    result = layer_norm(mixed_sum, outer_vectors[4], outer_vectors[5])
    maxima = lax.pmax(peak_logit, ("shard", "ctx"))
    positions = ctx_index * ctx_tokens + jnp.arange(ctx_tokens, dtype=jnp.int32)
    row_valid = (positions[None, :] < lengths[:, None]).astype(jnp.float32).reshape(-1)
    d_result = cotangent.reshape(-1, D).astype(jnp.float32) * row_valid[:, None]
    regathered = lax.all_gather(
        master_blocks.astype(jnp.bfloat16), ("shard", "ctx"), axis=0, tiled=True
    )
    wb_qkv, wb_out, wb_up, wb_down = unpack_weights(regathered, head_cols, unit_count)
    _, back_second = jax.vjp(layer_norm, mixed_sum, outer_vectors[4], outer_vectors[5])
    d_mixed, d_gain2, d_shift2 = back_second(d_result)
    d_ff_low = d_mixed.astype(jnp.bfloat16)
    d_bias2 = jnp.sum(d_ff_low.astype(jnp.float32), axis=0)
    g_down = jnp.dot(act_low.T, d_ff_low, preferred_element_type=jnp.float32)
    d_act = jnp.dot(d_ff_low, wb_down.T, preferred_element_type=jnp.float32)
    _, back_gelu = jax.vjp(gelu_tanh, gate_pre)
    d_gate_low = back_gelu(d_act)[0].astype(jnp.bfloat16)
    d_upbias = jnp.sum(d_gate_low.astype(jnp.float32), axis=0)
    g_up = jnp.dot(x_first_low.T, d_gate_low, preferred_element_type=jnp.float32)
    d_first = d_mixed + lax.psum(
        jnp.dot(d_gate_low, wb_up.T, preferred_element_type=jnp.float32), "tp"
    )
    _, back_first = jax.vjp(layer_norm, hidden_in, outer_vectors[2], outer_vectors[3])
    d_hidden, d_gain1, d_shift1 = back_first(d_first)
    d_branch_low = d_hidden.astype(jnp.bfloat16)
    d_bias_out = jnp.sum(d_branch_low.astype(jnp.float32), axis=0)
    g_out = jnp.dot(attended_low.T, d_branch_low, preferred_element_type=jnp.float32)
    d_att_low = jnp.dot(d_branch_low, wb_out.T, preferred_element_type=jnp.float32).astype(
        jnp.bfloat16
    )
    d_att_slots = d_att_low.reshape(slot_count, ctx_tokens, head_cols)
    keys_back, values_back = (keys_all, values_all)
    slot_index = 0
    clipped, key_mask = layouts[slot_index]
    query_blocks = query_slots[slot_index].reshape(rows_blocks, BLOCK, heads_here, HEAD)
    d_out_blocks = d_att_slots[slot_index].reshape(rows_blocks, BLOCK, heads_here, HEAD)
    d_query, d_key_full, d_value_full = group_back(
        query_blocks,
        d_out_blocks,
        keys_back[slot_index],
        values_back[slot_index],
        clipped,
        key_mask,
        lse_list[slot_index],
        None,
        block_count,
    )
    dk_list = [d_key_full]
    dv_list = [d_value_full]
    d_keys, d_values = (
        lax.psum_scatter(
            jnp.stack(dk_list).astype(jnp.bfloat16), "ctx", scatter_dimension=1, tiled=True
        ).astype(jnp.float32),
        lax.psum_scatter(
            jnp.stack(dv_list).astype(jnp.bfloat16), "ctx", scatter_dimension=1, tiled=True
        ).astype(jnp.float32),
    )
    d_q_low = d_query.astype(jnp.bfloat16)
    d_k_low = d_keys.reshape(-1, head_cols).astype(jnp.bfloat16)
    d_v_low = d_values.reshape(-1, head_cols).astype(jnp.bfloat16)
    d_proj = jnp.concatenate([d_q_low, d_k_low, d_v_low], axis=1)
    d_qbias = jnp.sum(d_q_low.astype(jnp.float32), axis=0)
    d_vbias = jnp.sum(d_v_low.astype(jnp.float32), axis=0)
    g_qkv = jnp.dot(flat_in.T, d_proj, preferred_element_type=jnp.float32)
    d_inputs = d_hidden + lax.psum(
        jnp.dot(d_proj, wb_qkv.T, preferred_element_type=jnp.float32).astype(jnp.bfloat16), "tp"
    ).astype(jnp.float32)
    input_grad = d_inputs.reshape(inputs.shape).astype(jnp.bfloat16)
    blocks_grad = jnp.concatenate(
        [from_grid(g_qkv), from_grid(g_out), from_grid(g_up), from_grid(g_down)], axis=0
    )
    outer_part = jnp.stack([d_bias_out, d_bias2, d_gain1, d_shift1, d_gain2, d_shift2], axis=0)
    inner_part = jnp.concatenate([d_qbias, d_vbias, d_upbias])[None, :]
    block_sum, outer_sum, inner_sum = (
        lax.psum_scatter(blocks_grad, ("shard", "ctx"), scatter_dimension=0, tiled=True),
        lax.psum_scatter(outer_part, ("shard", "ctx"), scatter_dimension=1, tiled=True),
        lax.psum_scatter(inner_part, ("shard", "ctx"), scatter_dimension=1, tiled=True),
    )
    left_new = 0.5 * left_stats + 0.5 * jnp.einsum(
        "bij,bkj->bik", block_sum, block_sum, precision=high
    )
    right_new = 0.5 * right_stats + 0.5 * jnp.einsum(
        "bji,bjk->bik", block_sum, block_sum, precision=high
    )
    left_applied = jnp.einsum("bij,bjk->bik", left_roots, block_sum, precision=high)
    step_val = jnp.einsum("bij,bjk->bik", left_applied, right_roots, precision=high)
    clip_sqrt = jnp.sqrt(tau_clip / jnp.maximum(maxima, tau_clip))
    head_factor = jnp.repeat(clip_sqrt, HEAD)
    table = jnp.concatenate([head_factor, head_factor, jnp.ones((head_cols,), jnp.float32)])
    qkv_factor = jnp.tile(table.reshape(1, -1, PB), (D // PB, 1, 1)).reshape(-1, PB)
    blocks_here = master_blocks.shape[0]
    all_factor = jnp.concatenate(
        [qkv_factor, jnp.ones((blocks_here * owner_count - qkv_factor.shape[0], PB), jnp.float32)],
        axis=0,
    )
    own_factor = lax.dynamic_slice_in_dim(all_factor, owner_index * blocks_here, blocks_here, 0)
    new_blocks = (master_blocks - rate_matrix * step_val) * own_factor[:, None, :]
    outer_cols = D // owner_count
    own_outer = lax.dynamic_slice_in_dim(outer_vectors, owner_index * outer_cols, outer_cols, 1)
    new_outer = own_outer - rate_vector * outer_sum
    inner_cols = inner_biases.shape[1] // owner_count
    inner_factor = jnp.concatenate([head_factor, jnp.ones((head_cols + unit_count,), jnp.float32)])
    own_inner_factor = lax.dynamic_slice_in_dim(
        inner_factor, owner_index * inner_cols, inner_cols, 0
    )
    own_inner = lax.dynamic_slice_in_dim(inner_biases, owner_index * inner_cols, inner_cols, 1)
    new_inner = (own_inner - rate_vector * inner_sum) * own_inner_factor[None, :]
    output = result.reshape(inputs.shape).astype(jnp.bfloat16)
    return (
        output,
        input_grad,
        block_sum,
        outer_sum,
        inner_sum,
        maxima,
        left_new,
        right_new,
        new_blocks,
        new_outer,
        new_inner,
    )


def solution(mesh):
    return jax.shard_map(
        per_device,
        mesh=mesh,
        in_specs=(
            P("shard", "ctx", None),
            P("shard"),
            P("shard", None),
            P("shard", "ctx", None),
            P(("shard", "ctx", "tp"), None, None),
            P(),
            P("tp", None),
            P(("shard", "ctx", "tp"), None, None),
            P(("shard", "ctx", "tp"), None, None),
            P(("shard", "ctx", "tp"), None, None),
            P(("shard", "ctx", "tp"), None, None),
            P("shard", "ctx", None),
        ),
        out_specs=(
            P("shard", "ctx", None),
            P("shard", "ctx", None),
            P(("shard", "ctx", "tp"), None, None),
            P(None, ("shard", "ctx")),
            P("tp", ("shard", "ctx")),
            P("tp"),
            P(("shard", "ctx", "tp"), None, None),
            P(("shard", "ctx", "tp"), None, None),
            P(("shard", "ctx", "tp"), None, None),
            P(None, ("shard", "ctx")),
            P("tp", ("shard", "ctx")),
        ),
        check_vma=False,
    )
```

profile of v0, /device:TPU:0, one launch (start us, length us, event | category | flops | bytes accessed | tf_op | source)
XLA Modules:
  0.0 1027.7 jit_solution(3224889106006550222)
XLA Ops:
  9.6 83.2 %all-gather.6.cloned.1.call-done = bf16[192,96,96]{2,1,0:T(8,128)(2,1)} async-done(((bf16[24,96,96]{2,1,0:T(8,128)(2,1)}), bf16[192,96,96]{2,1,0:T(8,128)(2,1)}) %all-gather.6.cloned.1.call-update) | async-done | bytes 3538960 | tf_op jit(solution)/shard_map/all_gather | solution.py:165
  109.1 27.4 %all-gather.10.cloned.1.call-done = bf16[4096,192]{0,1:T(8,128)(2,1)} async-done(((bf16[1024,192]{0,1:T(8,128)(2,1)}), bf16[4096,192]{0,1:T(8,128)(2,1)}) %all-gather.10.cloned.1.call-update) | async-done | bytes 1572880 | tf_op jit(solution)/shard_map/all_gather | solution.py:187
  142.4 15.9 %reshape.559 = bf16[16,512,3,64]{3,2,1,0:T(4,128)(2,1)} reshape(bf16[128,64,192]{2,1,0:T(8,128)(2,1)} %gather_fusion.1) | data formatting | bytes 6291456 | tf_op jit(solution)/shard_map/reshape | solution.py:73
  158.4 12.2 %copy.106 = bf16[16,512,3,64]{1,3,2,0:T(8,128)(2,1)} copy(bf16[16,512,3,64]{3,2,1,0:T(4,128)(2,1)} %reshape.559) | data formatting | bytes 6291456 | tf_op jit(solution)/shard_map/reshape | solution.py:73
  180.5 15.9 %reshape.558 = bf16[16,512,3,64]{3,2,1,0:T(4,128)(2,1)} reshape(bf16[128,64,192]{2,1,0:T(8,128)(2,1)} %gather_fusion) | data formatting | bytes 6291456 | tf_op jit(solution)/shard_map/reshape | solution.py:73
  196.4 12.3 %copy.107 = bf16[16,512,3,64]{1,3,2,0:T(8,128)(2,1)} copy(bf16[16,512,3,64]{3,2,1,0:T(4,128)(2,1)} %reshape.558) | data formatting | bytes 6291456 | tf_op jit(solution)/shard_map/reshape | solution.py:73
  237.2 52.6 %all-reduce.7.cloned.1.call-done = f32[1024,768]{1,0:T(8,128)} async-done(((f32[1024,768]{1,0:T(8,128)}), f32[1024,768]{1,0:T(8,128)}) %all-reduce.7.cloned.1.call-update) | async-done | bytes 3145744 | tf_op jit(solution)/shard_map/psum | solution.py:225
  302.4 67.8 %all-reduce.9.cloned.1.call-done = f32[1024,768]{1,0:T(8,128)} async-done(((f32[1024,768]{1,0:T(8,128)}), f32[1024,768]{1,0:T(8,128)}) %all-reduce.9.cloned.1.call-update) | async-done | bytes 3145744 | tf_op jit(solution)/shard_map/psum | solution.py:234
  393.6 67.9 %all-reduce.11.cloned.1.call-done = f32[1024,768]{1,0:T(8,128)} async-done(((f32[1024,768]{1,0:T(8,128)}), f32[1024,768]{1,0:T(8,128)}) %all-reduce.11.cloned.1.call-update) | async-done | bytes 3145744 | tf_op jit(solution)/shard_map/psum | solution.py:257
  461.5 5.4 multiply_reduce_fusion.1
  473.4 7.2 fusion.20
  480.6 15.1 %copy.136 = f32[16,512,3,64]{3,2,1,0:T(4,128)} copy(f32[16,512,3,64]{1,3,2,0:T(8,128)} %fusion.20) | data formatting | bytes 12582912 | tf_op jit(solution)/shard_map/reshape | solution.py:132
  495.7 18.9 %reshape.553 = f32[128,64,192]{2,1,0:T(8,128)} reshape(f32[16,512,3,64]{3,2,1,0:T(4,128)} %copy.136) | data formatting | bytes 12582912 | tf_op jit(solution)/shard_map/reshape | solution.py:132
  517.0 26.2 %scatter_fusion.1 = f32[64,64,192]{2,1,0:T(8,128)} fusion(f32[64,64,192]{2,1,0:T(8,128)} %broadcast.358.clone, s32[128]{0:T(128)S(1)} %reshape.508, f32[128,64,192]{2,1,0:T(8,128)} %reshape.553), kind=kCustom, calls=%fused_computation.3 | custom fusion | flops 1572864 | bytes 18874880 | tf_op jit(solution)/shard_map/scatter-add | solution.py:132
  548.7 6.7 multiply_reduce_fusion
  564.5 15.1 %copy.135 = f32[16,512,3,64]{3,2,1,0:T(4,128)} copy(f32[16,512,3,64]{1,3,2,0:T(8,128)} %multiply_bitcast_fusion) | data formatting | bytes 12582912 | tf_op jit(solution)/shard_map/reshape | solution.py:127
  579.6 18.9 %reshape.552 = f32[128,64,192]{2,1,0:T(8,128)} reshape(f32[16,512,3,64]{3,2,1,0:T(4,128)} %copy.135) | data formatting | bytes 12582912 | tf_op jit(solution)/shard_map/reshape | solution.py:127
  601.0 26.2 %scatter_fusion = f32[64,64,192]{2,1,0:T(8,128)} fusion(f32[64,64,192]{2,1,0:T(8,128)} %broadcast.358.clone.1, s32[128]{0:T(128)S(1)} %reshape.508, f32[128,64,192]{2,1,0:T(8,128)} %reshape.552), kind=kCustom, calls=%fused_computation.2 | custom fusion | flops 1572864 | bytes 18874880 | tf_op jit(solution)/shard_map/scatter-add | solution.py:127
  681.3 7.7 pad_maximum_fusion
  689.7 19.4 %pmax.7 = f32[3]{0:T(128)S(1)} all-reduce(f32[3]{0:T(128)S(1)} %broadcast_maximum_fusion), channel_id=1, replica_groups=mesh['shard'=2,'ctx'=4,'tp'=4] {'shard','ctx'}, use_global_device_ids=true, to_apply=%region_32.33 | all-reduce | flops 3 | bytes 24 | tf_op jit(solution)/shard_map/pmax | solution.py:239
  710.0 22.3 %reduce-scatter.16.cloned.1.call-done = f32[96,6]{1,0:T(8,128)} async-done(((f32[768,6]{1,0:T(8,128)}), f32[96,6]{1,0:T(8,128)}) %reduce-scatter.16.cloned.1.call-update) | async-done | bytes 2320
  734.6 63.3 %reduce-scatter.18.cloned.1.call-done = f32[144,1]{1,0:T(8,128)} async-done(((f32[1152,1]{1,0:T(8,128)}), f32[144,1]{1,0:T(8,128)}) %reduce-scatter.18.cloned.1.call-update) | async-done | bytes 592
  800.1 42.6 %all-reduce.13.cloned.1.call-done = bf16[1024,768]{1,0:T(8,128)(2,1)} async-done(((bf16[1024,768]{1,0:T(8,128)(2,1)}), bf16[1024,768]{1,0:T(8,128)(2,1)}) %all-reduce.13.cloned.1.call-update) | async-done | bytes 1572880 | tf_op jit(solution)/shard_map/psum | solution.py:302
  846.7 162.3 %reduce-scatter.14.cloned.1.call-done = f32[24,96,96]{2,1,0:T(8,128)} async-done(((f32[192,96,96]{2,1,0:T(8,128)}), f32[24,96,96]{2,1,0:T(8,128)}) %reduce-scatter.14.cloned.1.call-update) | async-done | bytes 884752 | tf_op jit(solution)/shard_map/reduce_scatter | solution.py:312
  (325 shorter events, 199.4 us)
Async XLA Ops:
  7.2 1001.7 %copy-start = (f32[24,96,96]{2,1,0:T(8,128)S(1)}, f32[24,96,96]{2,1,0:T(8,128)}, u32[]{:S(2)}) copy-start(f32[24,96,96]{2,1,0:T(8,128)} %param.21) | copy-start | bytes 2654212
  7.2 85.6 %all-gather.6.cloned.1.call-start = ((), (), s32[]{:S(2)}) async-start(), calls=%async_computation.5 | async-start | bytes 5308416 | tf_op jit(solution)/shard_map/all_gather | solution.py:165
  9.5 127.0 %all-gather.10.cloned.1.call-start = ((), (), s32[]{:S(2)}) async-start(), calls=%async_computation.14 | async-start | bytes 1966080 | tf_op jit(solution)/shard_map/all_gather | solution.py:187
  101.0 73.7 %all-gather.8.cloned.1.call-start = ((), (), s32[]{:S(2)}) async-start(), calls=%async_computation.13 | async-start | bytes 1966080 | tf_op jit(solution)/shard_map/all_gather | solution.py:188
  103.4 186.4 %all-reduce.7.cloned.1.call-start = ((), (), s32[]{:S(2)}) async-start(), calls=%async_computation.6 | async-start | bytes 6291456 | tf_op jit(solution)/shard_map/psum | solution.py:225
  222.3 147.8 %all-reduce.9.cloned.1.call-start = ((), (), s32[]{:S(2)}) async-start(), calls=%async_computation.7 | async-start | bytes 6291456 | tf_op jit(solution)/shard_map/psum | solution.py:234
  223.9 68.9 %copy-start.43 = (f32[768]{0:T(1024)}, f32[768]{0:T(1024)S(1)}, u32[]{:S(2)}) copy-start(f32[768]{0:T(1024)S(1)} %get-tuple-element.22) | copy-start | bytes 9220
  223.9 68.9 %copy-start.49 = (f32[768]{0:T(1024)}, f32[768]{0:T(1024)S(1)}, u32[]{:S(2)}) copy-start(f32[768]{0:T(1024)S(1)} %get-tuple-element.21) | copy-start | bytes 9220
  233.3 56.5 %copy-start.23 = (bf16[1,1024,768]{2,1,0:T(8,128)(2,1)S(1)}, bf16[1,1024,768]{2,1,0:T(8,128)(2,1)}, u32[]{:S(2)}) copy-start(bf16[1,1024,768]{2,1,0:T(8,128)(2,1)} %param.12) | copy-start | bytes 4718596
  301.5 160.0 %all-reduce.11.cloned.1.call-start = ((), (), s32[]{:S(2)}) async-start(), calls=%async_computation.8 | async-start | bytes 6291456 | tf_op jit(solution)/shard_map/psum | solution.py:257
  392.8 68.7 %copy-start.42 = (f32[1024]{0:T(1024)S(1)}, f32[1024]{0:T(1024)}, u32[]{:S(2)}) copy-start(f32[1024]{0:T(1024)} %copy-done.41) | copy-start | bytes 12292
  392.8 68.7 %copy-start.44 = (f32[768]{0:T(1024)S(1)}, f32[768]{0:T(1024)}, u32[]{:S(2)}) copy-start(f32[768]{0:T(1024)} %copy-done.43) | copy-start | bytes 9220
  392.8 68.7 %copy-start.46 = (f32[1024]{0:T(1024)S(1)}, f32[1024]{0:T(1024)}, u32[]{:S(2)}) copy-start(f32[1024]{0:T(1024)} %copy-done.45) | copy-start | bytes 12292
  392.8 269.5 %reduce-scatter.12.cloned.1.call-start = ((), (), s32[]{:S(2)}) async-start(), calls=%async_computation.10 | async-start | bytes 1966080 | tf_op jit(solution)/shard_map/reduce_scatter | solution.py:291
  393.6 73.3 %copy-start.51 = (f32[1024]{0:T(1024)S(1)}, f32[1024]{0:T(1024)}, u32[]{:S(2)}) copy-start(f32[1024]{0:T(1024)} %copy-done.50) | copy-start | bytes 12292
  548.4 119.6 %reduce-scatter.10.cloned.1.call-start = ((), (), s32[]{:S(2)}) async-start(), calls=%async_computation.9 | async-start | bytes 1966080 | tf_op jit(solution)/shard_map/reduce_scatter | solution.py:288
  632.4 99.9 %reduce-scatter.16.cloned.1.call-start = ((), (), s32[]{:S(2)}) async-start(), calls=%async_computation.15 | async-start | bytes 442368
  662.2 135.6 %reduce-scatter.18.cloned.1.call-start = ((), (), s32[]{:S(2)}) async-start(), calls=%async_computation.16 | async-start | bytes 663552
  664.6 178.1 %all-reduce.13.cloned.1.call-start = ((), (), s32[]{:S(2)}) async-start(), calls=%async_computation.11 | async-start | bytes 3145728 | tf_op jit(solution)/shard_map/psum | solution.py:302
  672.1 336.8 %reduce-scatter.14.cloned.1.call-start = ((), (), s32[]{:S(2)}) async-start(), calls=%async_computation.12 | async-start | bytes 10616832 | tf_op jit(solution)/shard_map/reduce_scatter | solution.py:312
  733.2 109.5 %copy-start.58 = (f32[6,96]{1,0:T(8,128)}, f32[6,96]{1,0:T(8,128)S(1)}, u32[]{:S(2)}) copy-start(f32[6,96]{1,0:T(8,128)S(1)} %copy.138) | copy-start | bytes 6916
  798.8 43.9 %copy-start.66 = (f32[1,144]{1,0:T(1,128)}, f32[1,144]{1,0:T(1,128)S(1)}, u32[]{:S(2)}) copy-start(f32[1,144]{1,0:T(1,128)S(1)} %copy.140) | copy-start | bytes 1732
  846.7 164.8 %copy-start.18 = (f32[24,96,96]{2,1,0:T(8,128)S(1)}, f32[24,96,96]{2,1,0:T(8,128)}, u32[]{:S(2)}) copy-start(f32[24,96,96]{2,1,0:T(8,128)} %param.16) | copy-start | bytes 2654212
  846.7 164.8 %copy-start.27 = (f32[24,96,96]{2,1,0:T(8,128)S(1)}, f32[24,96,96]{2,1,0:T(8,128)}, u32[]{:S(2)}) copy-start(f32[24,96,96]{2,1,0:T(8,128)} %param.22) | copy-start | bytes 2654212
  (69 other events, 245.1 us)
Sparse Core Ops, SparseCore 0:
  10.7 82.0 all-gather.5
  101.1 35.3 all-gather.9
  138.7 35.9 all-gather.7
  222.5 67.2 all-reduce.6
  301.6 68.5 all-reduce.8
  392.9 68.5 all-reduce.10
  548.5 35.4 reduce-scatter.11
  632.5 35.4 reduce-scatter.9
  671.3 61.0 reduce-scatter.15
  736.0 61.7 reduce-scatter.17
  800.8 41.8 all-reduce.12
  846.7 162.1 reduce-scatter.13
where the time goes:
time: 1030 us
  waiting for transfers between devices  597 us (58%)
  local copies, waits for them, and re-layouts  215 us (21%)
  other arithmetic  108 us (10%)
  matrix products  69.6 us (7%)
  blocking collectives  19.4 us (2%)
  between operations  16.1 us (2%)
    reduce_scatter x1, waiting for transfers between devices, per_device(): lax.psum_scatter(blocks_grad, ('shard', 'ctx'), scatter_dimension=0, tile...  162 us
    unnamed x14, waiting for transfers between devices  85.7 us
    all_gather x1, waiting for transfers between devices, per_device(): lax.all_gather(master_blocks.astype(jnp.bfloat16), ('shard', 'ctx'), axis...  83.2 us
    psum x1, waiting for transfers between devices, per_device(): lax.psum(jnp.dot(d_gate_low, wb_up.T, preferred_element_type=jnp.float32)...  67.9 us
    psum x1, waiting for transfers between devices, per_device(): lax.psum(jnp.dot(act_low, w_down, preferred_element_type=jnp.float32), 'tp')  67.8 us
    reshape x4, local copies, waits for them, and re-layouts, pick_blocks(): picked.reshape(clipped.shape[0], clipped.shape[1] * BLOCK, head_count, HEAD)  56.3 us
    psum x1, waiting for transfers between devices, per_device(): lax.psum(jnp.dot(attended_low, w_out, preferred_element_type=jnp.float32)...  52.6 us
    psum x1, waiting for transfers between devices, per_device(): lax.psum(jnp.dot(d_proj, wb_qkv.T, preferred_element_type=jnp.float32).as...  42.6 us
  transfers between devices with their start and end apart: 12, of which 11 were waited for; matrix products, arithmetic and copies ran while one was open for 19% of the time, Pallas kernels for 0%

commit v1 on v0

--- a/solution.py
+++ b/solution.py
@@ -16,6 +16,18 @@
 rate_vector = 0.001
 neg_large = -1e30
 high = lax.Precision.HIGHEST
+
+
+def collect(shard, axis, dim):
+    ways, here, turn = (lax.axis_size(axis), lax.axis_index(axis), shard.shape[dim])
+    line, have = (shard, 1)
+    while have < ways:
+        line = jnp.concatenate(
+            [line, lax.ppermute(line, axis, [(d, (d - have) % ways) for d in range(ways)])],
+            axis=dim,
+        )
+        have = 2 * have
+    return jnp.roll(line, here * turn, axis=dim)
 
 
 def layer_norm(values, gain, shift):
@@ -162,9 +174,7 @@
     block_count = SEQ // BLOCK
     ctx_index = lax.axis_index("ctx")
     owner_index = lax.axis_index(("shard", "ctx"))
-    gathered = lax.all_gather(
-        master_blocks.astype(jnp.bfloat16), ("shard", "ctx"), axis=0, tiled=True
-    )
+    gathered = collect(master_blocks.astype(jnp.bfloat16), ("shard", "ctx"), 0)
     w_qkv, w_out, w_up, w_down = unpack_weights(gathered, head_cols, unit_count)
     flat_in = inputs.reshape(-1, D)
     inner_row = inner_biases[0]

time: 1030 us -> 1090 us (1.058)
  local copies, waits for them, and re-layouts: 215 us -> 244 us
  waiting for transfers between devices: 597 us -> 613 us
    ppermute x0 -> x3, waiting for transfers between devices: none -> 114 us  [collect(): lax.ppermute(line, axis, [(d, (d - have) % ways) for d in range(ways)])]
    all_gather x1, waiting for transfers between devices: 83.2 us -> 1.37 us  [per_device(): lax.all_gather(master_blocks.astype(jnp.bfloat16), ('shard', 'ctx'), axis...]
    psum x1, waiting for transfers between devices: 67.8 us -> 54.6 us  [per_device(): lax.psum(jnp.dot(act_low, w_down, preferred_element_type=jnp.float32), 'tp')]
    unnamed x164 -> x124, local copies, waits for them, and re-layouts: 19.5 us -> 27.9 us
  transfers between devices with their start and end apart: 12 -> 15, of which waited for: 11 -> 14; matrix products, arithmetic and copies ran while one was open for 19% -> 21% of each run, Pallas kernels for 0% -> 0%
where the time goes in v1:
time: 1090 us; the launch traced here: 1080 us
  waiting for transfers between devices  613 us (56%)
  local copies, waits for them, and re-layouts  244 us (22%)
  other arithmetic  110 us (10%)
  matrix products  69.1 us (6%)
  blocking collectives  21.1 us (2%)
  between operations  17 us (2%)
    reduce_scatter x1, waiting for transfers between devices, per_device(): lax.psum_scatter(blocks_grad, ('shard', 'ctx'), scatter_dimension=0, tile...  162 us
    ppermute x3, waiting for transfers between devices, collect(): lax.ppermute(line, axis, [(d, (d - have) % ways) for d in range(ways)])  114 us
    unnamed x14, waiting for transfers between devices  85.4 us
    psum x1, waiting for transfers between devices, per_device(): lax.psum(jnp.dot(d_gate_low, wb_up.T, preferred_element_type=jnp.float32)...  67.2 us
    reshape x4, local copies, waits for them, and re-layouts, pick_blocks(): picked.reshape(clipped.shape[0], clipped.shape[1] * BLOCK, head_count, HEAD)  56.3 us
    psum x1, waiting for transfers between devices, per_device(): lax.psum(jnp.dot(attended_low, w_out, preferred_element_type=jnp.float32)...  56 us
    psum x1, waiting for transfers between devices, per_device(): lax.psum(jnp.dot(act_low, w_down, preferred_element_type=jnp.float32), 'tp')  54.6 us
    psum x1, waiting for transfers between devices, per_device(): lax.psum(jnp.dot(d_proj, wb_qkv.T, preferred_element_type=jnp.float32).as...  42.4 us
  transfers between devices with their start and end apart: 15, of which 14 were waited for; matrix products, arithmetic and copies ran while one was open for 21% of the time, Pallas kernels for 0%

profile of v1, /device:TPU:0, one launch (start us, length us, event | category | flops | bytes accessed | tf_op | source)
XLA Modules:
  0.0 1084.3 jit_solution(11033030616503704753)
XLA Ops:
  16.4 12.6 %collective-permute-done = bf16[24,96,96]{2,1,0:T(8,128)(2,1)S(1)} collective-permute-done((bf16[24,96,96]{2,1,0:T(8,128)(2,1)S(1)}, bf16[24,96,96]{2,1,0:T(8,128)(2,1)S(1)}, u32[]{:S(2)}, u32[]{:S(2)}) %collective-permute-start) | collective-permute-done | bytes 442400 | tf_op jit(solution)/shard_map/ppermute | solution.py:26
  30.8 51.6 %collective-permute-done.1 = bf16[48,96,96]{2,1,0:T(8,128)(2,1)S(1)} collective-permute-done((bf16[48,96,96]{2,1,0:T(8,128)(2,1)S(1)}, bf16[48,96,96]{2,1,0:T(8,128)(2,1)S(1)}, u32[]{:S(2)}, u32[]{:S(2)}) %collective-permute-start.1) | collective-permute-done | bytes 884768 | tf_op jit(solution)/shard_map/ppermute | solution.py:26
  86.8 49.4 %collective-permute-done.2 = bf16[96,96,96]{2,1,0:T(8,128)(2,1)} collective-permute-done((bf16[96,96,96]{2,1,0:T(8,128)(2,1)}, bf16[96,96,96]{2,1,0:T(8,128)(2,1)}, u32[]{:S(2)}, u32[]{:S(2)}) %collective-permute-start.2) | collective-permute-done | bytes 1769504 | tf_op jit(solution)/shard_map/ppermute | solution.py:26
  166.9 25.1 %all-gather.10.cloned.1.call-done = bf16[4096,192]{0,1:T(8,128)(2,1)} async-done(((bf16[1024,192]{0,1:T(8,128)(2,1)}), bf16[4096,192]{0,1:T(8,128)(2,1)}) %all-gather.10.cloned.1.call-update) | async-done | bytes 1572880 | tf_op jit(solution)/shard_map/all_gather | solution.py:197
  198.0 15.9 %reshape.583 = bf16[16,512,3,64]{3,2,1,0:T(4,128)(2,1)} reshape(bf16[128,64,192]{2,1,0:T(8,128)(2,1)} %gather_fusion.1) | data formatting | bytes 6291456 | tf_op jit(solution)/shard_map/reshape | solution.py:85
  213.9 12.2 %copy.114 = bf16[16,512,3,64]{1,3,2,0:T(8,128)(2,1)} copy(bf16[16,512,3,64]{3,2,1,0:T(4,128)(2,1)} %reshape.583) | data formatting | bytes 6291456 | tf_op jit(solution)/shard_map/reshape | solution.py:85
  236.1 15.9 %reshape.582 = bf16[16,512,3,64]{3,2,1,0:T(4,128)(2,1)} reshape(bf16[128,64,192]{2,1,0:T(8,128)(2,1)} %gather_fusion) | data formatting | bytes 6291456 | tf_op jit(solution)/shard_map/reshape | solution.py:85
  251.9 12.3 %copy.115 = bf16[16,512,3,64]{1,3,2,0:T(8,128)(2,1)} copy(bf16[16,512,3,64]{3,2,1,0:T(4,128)(2,1)} %reshape.582) | data formatting | bytes 6291456 | tf_op jit(solution)/shard_map/reshape | solution.py:85
  289.2 56.0 %all-reduce.7.cloned.1.call-done = f32[1024,768]{1,0:T(8,128)} async-done(((f32[1024,768]{1,0:T(8,128)}), f32[1024,768]{1,0:T(8,128)}) %all-reduce.7.cloned.1.call-update) | async-done | bytes 3145744 | tf_op jit(solution)/shard_map/psum | solution.py:235
  371.3 54.6 %all-reduce.9.cloned.1.call-done = f32[1024,768]{1,0:T(8,128)} async-done(((f32[1024,768]{1,0:T(8,128)}), f32[1024,768]{1,0:T(8,128)}) %all-reduce.9.cloned.1.call-update) | async-done | bytes 3145744 | tf_op jit(solution)/shard_map/psum | solution.py:244
  450.3 67.2 %all-reduce.11.cloned.1.call-done = f32[1024,768]{1,0:T(8,128)} async-done(((f32[1024,768]{1,0:T(8,128)}), f32[1024,768]{1,0:T(8,128)}) %all-reduce.11.cloned.1.call-update) | async-done | bytes 3145744 | tf_op jit(solution)/shard_map/psum | solution.py:267
  528.8 7.2 fusion.20
  536.0 15.1 %copy.148 = f32[16,512,3,64]{3,2,1,0:T(4,128)} copy(f32[16,512,3,64]{1,3,2,0:T(8,128)} %fusion.20) | data formatting | bytes 12582912 | tf_op jit(solution)/shard_map/reshape | solution.py:144
  551.1 18.9 %reshape.577 = f32[128,64,192]{2,1,0:T(8,128)} reshape(f32[16,512,3,64]{3,2,1,0:T(4,128)} %copy.148) | data formatting | bytes 12582912 | tf_op jit(solution)/shard_map/reshape | solution.py:144
  572.4 26.1 %scatter_fusion.1 = f32[64,64,192]{2,1,0:T(8,128)} fusion(f32[64,64,192]{2,1,0:T(8,128)} %broadcast.358.clone, s32[128]{0:T(128)S(1)} %reshape.532, f32[128,64,192]{2,1,0:T(8,128)} %reshape.577), kind=kCustom, calls=%fused_computation.3 | custom fusion | flops 1572864 | bytes 18874880 | tf_op jit(solution)/shard_map/scatter-add | solution.py:144
  619.7 15.1 %copy.147 = f32[16,512,3,64]{3,2,1,0:T(4,128)} copy(f32[16,512,3,64]{1,3,2,0:T(8,128)} %multiply_bitcast_fusion) | data formatting | bytes 12582912 | tf_op jit(solution)/shard_map/reshape | solution.py:139
  634.8 18.9 %reshape.576 = f32[128,64,192]{2,1,0:T(8,128)} reshape(f32[16,512,3,64]{3,2,1,0:T(4,128)} %copy.147) | data formatting | bytes 12582912 | tf_op jit(solution)/shard_map/reshape | solution.py:139
  656.2 26.2 %scatter_fusion = f32[64,64,192]{2,1,0:T(8,128)} fusion(f32[64,64,192]{2,1,0:T(8,128)} %broadcast.358.clone.1, s32[128]{0:T(128)S(1)} %reshape.532, f32[128,64,192]{2,1,0:T(8,128)} %reshape.576), kind=kCustom, calls=%fused_computation.2 | custom fusion | flops 1572864 | bytes 18874880 | tf_op jit(solution)/shard_map/scatter-add | solution.py:139
  736.9 7.7 pad_maximum_fusion
  745.2 21.1 %pmax.7 = f32[3]{0:T(128)S(1)} all-reduce(f32[3]{0:T(128)S(1)} %broadcast_maximum_fusion), channel_id=1, replica_groups=mesh['shard'=2,'ctx'=4,'tp'=4] {'shard','ctx'}, use_global_device_ids=true, to_apply=%region_32.33 | all-reduce | flops 3 | bytes 24 | tf_op jit(solution)/shard_map/pmax | solution.py:249
  767.3 21.3 %reduce-scatter.16.cloned.1.call-done = f32[96,6]{1,0:T(8,128)} async-done(((f32[768,6]{1,0:T(8,128)}), f32[96,6]{1,0:T(8,128)}) %reduce-scatter.16.cloned.1.call-update) | async-done | bytes 2320
  790.9 63.4 %reduce-scatter.18.cloned.1.call-done = f32[144,1]{1,0:T(8,128)} async-done(((f32[1152,1]{1,0:T(8,128)}), f32[144,1]{1,0:T(8,128)}) %reduce-scatter.18.cloned.1.call-update) | async-done | bytes 592
  856.5 42.4 %all-reduce.13.cloned.1.call-done = bf16[1024,768]{1,0:T(8,128)(2,1)} async-done(((bf16[1024,768]{1,0:T(8,128)(2,1)}), bf16[1024,768]{1,0:T(8,128)(2,1)}) %all-reduce.13.cloned.1.call-update) | async-done | bytes 1572880 | tf_op jit(solution)/shard_map/psum | solution.py:312
  902.9 162.4 %reduce-scatter.14.cloned.1.call-done = f32[24,96,96]{2,1,0:T(8,128)} async-done(((f32[192,96,96]{2,1,0:T(8,128)}), f32[24,96,96]{2,1,0:T(8,128)}) %reduce-scatter.14.cloned.1.call-update) | async-done | bytes 884752 | tf_op jit(solution)/shard_map/reduce_scatter | solution.py:322
  (305 shorter events, 248.7 us)
Async XLA Ops:
  8.0 1057.3 %copy-start = (f32[24,96,96]{2,1,0:T(8,128)S(1)}, f32[24,96,96]{2,1,0:T(8,128)}, u32[]{:S(2)}) copy-start(f32[24,96,96]{2,1,0:T(8,128)} %param.21) | copy-start | bytes 2654212
  8.0 184.0 %all-gather.10.cloned.1.call-start = ((), (), s32[]{:S(2)}) async-start(), calls=%async_computation.14 | async-start | bytes 1966080 | tf_op jit(solution)/shard_map/all_gather | solution.py:197
  10.4 129.1 %copy-start.7 = (bf16[24,96,96]{2,1,0:T(8,128)(2,1)}, bf16[24,96,96]{2,1,0:T(8,128)(2,1)S(1)}, u32[]{:S(2)}) copy-start(bf16[24,96,96]{2,1,0:T(8,128)(2,1)S(1)} %get-tuple-element.41) | copy-start | bytes 1327108
  10.4 18.6 %collective-permute-start = (bf16[24,96,96]{2,1,0:T(8,128)(2,1)S(1)}, bf16[24,96,96]{2,1,0:T(8,128)(2,1)S(1)}, u32[]{:S(2)}, u32[]{:S(2)}) collective-permute-start(bf16[24,96,96]{2,1,0:T(8,128)(2,1)S(1)} %get-tuple-element.41), channel_id=1, source_target_pairs={{0,28},{4,0},{8,4},{12,8},{16,12},{20,16},{24,20},{28,24},{1,29},{... | collective-permute-start | bytes 1327112 | tf_op jit(solution)/shard_map/ppermute | solution.py:26
  29.2 53.1 %collective-permute-start.1 = (bf16[48,96,96]{2,1,0:T(8,128)(2,1)S(1)}, bf16[48,96,96]{2,1,0:T(8,128)(2,1)S(1)}, u32[]{:S(2)}, u32[]{:S(2)}) collective-permute-start(bf16[48,96,96]{2,1,0:T(8,128)(2,1)S(1)} %pad_maximum_fusion.2), channel_id=1, source_target_pairs={{0,24},{4,28},{8,0},{12,4},{16,8},{20,12},{24,16},{28,20},{1,25},{... | collective-permute-start | bytes 2654216 | tf_op jit(solution)/shard_map/ppermute | solution.py:26
  84.3 51.9 %collective-permute-start.2 = (bf16[96,96,96]{2,1,0:T(8,128)(2,1)}, bf16[96,96,96]{2,1,0:T(8,128)(2,1)}, u32[]{:S(2)}, u32[]{:S(2)}) collective-permute-start(bf16[96,96,96]{2,1,0:T(8,128)(2,1)} %pad_maximum_fusion.1), channel_id=1, source_target_pairs={{0,16},{4,20},{8,24},{12,28},{16,0},{20,4},{24,8},{28,12},{1,17},{... | collective-permute-start | bytes 5308424 | tf_op jit(solution)/shard_map/ppermute | solution.py:26
  153.3 76.8 %all-gather.8.cloned.1.call-start = ((), (), s32[]{:S(2)}) async-start(), calls=%async_computation.13 | async-start | bytes 1966080 | tf_op jit(solution)/shard_map/all_gather | solution.py:198
  155.0 190.2 %all-reduce.7.cloned.1.call-start = ((), (), s32[]{:S(2)}) async-start(), calls=%async_computation.5 | async-start | bytes 6291456 | tf_op jit(solution)/shard_map/psum | solution.py:235
  251.9 12.3 %copy-start.13 = (bf16[16,64,3,64]{1,0,3,2:T(8,128)(2,1)S(1)}, bf16[16,64,3,64]{1,0,3,2:T(8,128)(2,1)}, u32[]{:S(2)}) copy-start(bf16[16,64,3,64]{1,0,3,2:T(8,128)(2,1)} %reshape_squeeze_reshape.7) | copy-start | bytes 1179652
  277.8 81.1 %all-gather.6.cloned.1.call-start = ((), (), s32[]{:S(2)}) async-start(), calls=%async_computation.7 | async-start | bytes 5308416 | tf_op jit(solution)/shard_map/all_gather | solution.py:253
  278.3 147.6 %all-reduce.9.cloned.1.call-start = ((), (), s32[]{:S(2)}) async-start(), calls=%async_computation.6 | async-start | bytes 6291456 | tf_op jit(solution)/shard_map/psum | solution.py:244
  278.9 157.7 %copy-start.48 = (f32[768]{0:T(1024)}, f32[768]{0:T(1024)S(1)}, u32[]{:S(2)}) copy-start(f32[768]{0:T(1024)S(1)} %slice_reduce_fusion.3) | copy-start | bytes 9220
  357.3 160.3 %all-reduce.11.cloned.1.call-start = ((), (), s32[]{:S(2)}) async-start(), calls=%async_computation.8 | async-start | bytes 6291456 | tf_op jit(solution)/shard_map/psum | solution.py:267
  436.3 8.2 copy-start.5
  448.9 271.8 %reduce-scatter.12.cloned.1.call-start = ((), (), s32[]{:S(2)}) async-start(), calls=%async_computation.10 | async-start | bytes 1966080 | tf_op jit(solution)/shard_map/reduce_scatter | solution.py:301
  603.7 120.0 %reduce-scatter.10.cloned.1.call-start = ((), (), s32[]{:S(2)}) async-start(), calls=%async_computation.9 | async-start | bytes 1966080 | tf_op jit(solution)/shard_map/reduce_scatter | solution.py:298
  687.7 100.9 %reduce-scatter.16.cloned.1.call-start = ((), (), s32[]{:S(2)}) async-start(), calls=%async_computation.15 | async-start | bytes 442368
  720.6 133.6 %reduce-scatter.18.cloned.1.call-start = ((), (), s32[]{:S(2)}) async-start(), calls=%async_computation.16 | async-start | bytes 663552
  723.0 175.9 %all-reduce.13.cloned.1.call-start = ((), (), s32[]{:S(2)}) async-start(), calls=%async_computation.11 | async-start | bytes 3145728 | tf_op jit(solution)/shard_map/psum | solution.py:312
  727.8 337.5 %reduce-scatter.14.cloned.1.call-start = ((), (), s32[]{:S(2)}) async-start(), calls=%async_computation.12 | async-start | bytes 10616832 | tf_op jit(solution)/shard_map/reduce_scatter | solution.py:322
  789.5 109.5 %copy-start.37 = (f32[6,96]{1,0:T(8,128)}, f32[6,96]{1,0:T(8,128)S(1)}, u32[]{:S(2)}) copy-start(f32[6,96]{1,0:T(8,128)S(1)} %copy.150) | copy-start | bytes 6916
  855.2 43.8 %copy-start.45 = (f32[1,144]{1,0:T(1,128)}, f32[1,144]{1,0:T(1,128)S(1)}, u32[]{:S(2)}) copy-start(f32[1,144]{1,0:T(1,128)S(1)} %copy.152) | copy-start | bytes 1732
  902.9 164.9 %copy-start.19 = (f32[24,96,96]{2,1,0:T(8,128)S(1)}, f32[24,96,96]{2,1,0:T(8,128)}, u32[]{:S(2)}) copy-start(f32[24,96,96]{2,1,0:T(8,128)} %param.16) | copy-start | bytes 2654212
  902.9 164.9 %copy-start.26 = (f32[24,96,96]{2,1,0:T(8,128)S(1)}, f32[24,96,96]{2,1,0:T(8,128)}, u32[]{:S(2)}) copy-start(f32[24,96,96]{2,1,0:T(8,128)} %param.22) | copy-start | bytes 2654212
  (49 other events, 162.0 us)
Sparse Core Ops, SparseCore 0:
  153.4 38.5 all-gather.9
  194.1 35.9 all-gather.7
  277.9 67.2 all-reduce.6
  357.4 68.5 all-reduce.8
  449.0 68.5 all-reduce.10
  603.8 35.7 reduce-scatter.11
  687.8 35.7 reduce-scatter.9
  727.5 61.0 reduce-scatter.15
  792.5 61.7 reduce-scatter.17
  857.0 41.8 all-reduce.12
  903.1 162.1 reduce-scatter.13
Sparse Core Ops, SparseCore 1:
  280.9 77.9 all-gather.5
